TPU v7x, 128 devices: a whole 4x4x4 slice. The times are simulated.
128 devices in a mesh: cell: 2 (over core), panel: 2 (over x_lo), sc: 32 (over z, y, x_hi).
Axes of the slice: x: 4 (x_hi: 2, x_lo: 2; x = x_hi * 2 + x_lo), y: 4, z: 4, core: 2. Of those that a mesh axis runs over, the one named last changes fastest.
Arguments:
- channel: bfloat16 [4, 1024, 2, 1024, 128], P('cell', 'sc', None, 'panel'), may hold values from -0.1875 to 0.1875
- received: bfloat16 [4, 1024, 2, 14, 1024], P('cell', 'sc', None, None, 'panel'), may hold values from -6 to 6
- noise_power: float32 [4], P('cell'), may hold values from 0.05 to 0.5
- user_count: int32 [4, 64], P('cell', 'sc'), may hold values from 32 to 128
- serving_cell: int32 [4, 128, 1], P('cell'), may hold values from 0 to 3; in each aligned block of 256 rows (0 to 255, 256 to 511, ..., all dimensions but the last counted through in order) at most 128 rows name the same one
Outputs:
- routed_symbols: bfloat16 [4, 256, 2, 14, 1024], P('cell', 'sc')
Inputs may be any that keep to these rules, and one draw needn't show every extreme that they name: `serving_cell`: at most 128 user slots of one block of 2 consecutive cells name the same serving cell, and in every draw some serving cell is named exactly 128 times by one block.
All inputs are finite; a program needn't handle non-finite values.
Results may differ from a plain program's by a relative error of at most 0.0057.
Values may be sent and summed in bfloat16 or wider, within the bound.
A program may use at most 128 MiB of HBM per device.

v0:
```python
import jax
import jax.numpy as jnp
from jax import lax
from jax.sharding import PartitionSpec as P

GRP = 16
ITERS = 2


def with_halo(block, sides, width):
    for axis, dim in sides:
        count = lax.axis_size(axis)
        forward = [(i, i + 1) for i in range(count - 1)]
        backward = [(target, source) for source, target in forward]
        low = lax.ppermute(
            lax.slice_in_dim(block, block.shape[dim] - width, None, axis=dim), axis, forward
        )
        high = lax.ppermute(lax.slice_in_dim(block, 0, width, axis=dim), axis, backward)
        block = jnp.concatenate([low, block, high], axis=dim)
    return block


def adjoint_apply(matrix, vector):
    products = jnp.einsum("cfaku,cfbsk->cfabsu", matrix, vector, preferred_element_type=jnp.float32)
    return jnp.stack(
        (products[:, :, 0, 0] + products[:, :, 1, 1], products[:, :, 0, 1] - products[:, :, 1, 0]),
        axis=2,
    )


def apply_channel(matrix, vector):
    products = jnp.einsum("cfaku,cfbsu->cfabsk", matrix, vector, preferred_element_type=jnp.float32)
    return jnp.stack(
        (products[:, :, 0, 0] - products[:, :, 1, 1], products[:, :, 0, 1] + products[:, :, 1, 0]),
        axis=2,
    )


def user_sum(left, right):
    return jnp.sum(left * right, axis=(2, 4))


def widen(values):
    return values[:, :, None, :, None]


def body(channel, received, noise_power, user_count, serving_cell):
    cells, band, _, antennas, users = channel.shape
    padded = with_halo(channel, (("sc", 1),), 1)
    total = band * lax.axis_size("sc")
    index = lax.axis_index("sc") * band + lax.iota(jnp.int32, band)
    weight = jnp.where((index == 0) | (index == total - 1), 0.75, 1.0).astype(jnp.float32)
    lower = padded[:, :-2].astype(jnp.float32)
    middle = padded[:, 1:-1].astype(jnp.float32)
    upper = padded[:, 2:].astype(jnp.float32)
    smooth = (0.25 * lower + 0.5 * middle + 0.25 * upper) / weight[None, :, None, None, None]
    counts = jnp.repeat(user_count, GRP, axis=1)
    active = (lax.iota(jnp.int32, users)[None, None, :] < counts[:, :, None]).astype(jnp.float32)
    smoothed = (smooth * active[:, :, None, None, :]).astype(jnp.bfloat16)
    partial_sums = adjoint_apply(smoothed, received)
    noise = noise_power[:, None, None, None, None]
    matched = lax.psum(partial_sums, "panel")
    estimate = jnp.zeros_like(matched)
    residual = matched
    direction = matched
    norm_now = user_sum(residual, residual)
    for iteration in range(ITERS):
        column_image = apply_channel(smoothed, direction.astype(jnp.bfloat16)).astype(jnp.bfloat16)
        image = lax.psum(adjoint_apply(smoothed, column_image), "panel") + noise * direction
        alpha = norm_now / user_sum(direction, image)
        estimate = estimate + widen(alpha) * direction
        residual = residual - widen(alpha) * image
        norm_next = user_sum(residual, residual)
        direction = residual + widen(norm_next / norm_now) * direction
        norm_now = norm_next
    detected = estimate.astype(jnp.bfloat16)
    n_cell = lax.axis_size("cell")
    capacity = 2 * users // n_cell
    slot_count = n_cell * capacity
    keys = serving_cell[:, :, 0].reshape(-1)
    position = lax.iota(jnp.int32, cells * users)
    earlier = (keys[:, None] == keys[None, :]) & (position[None, :] < position[:, None])
    rank = jnp.sum(earlier.astype(jnp.int32), axis=1)
    target = keys % cells * slot_count + keys // cells * capacity + rank
    onehot = (target[:, None] == lax.iota(jnp.int32, cells * slot_count)[None, :]).astype(
        jnp.bfloat16
    )
    onehot = onehot.reshape(cells, users, cells * slot_count)
    outgoing = jnp.einsum("cfasu,cut->tasf", detected, onehot, preferred_element_type=jnp.float32)
    outgoing = outgoing.astype(jnp.bfloat16).reshape(cells, slot_count, 2, detected.shape[3], band)
    return lax.all_to_all(
        lax.all_to_all(outgoing, "cell", split_axis=1, concat_axis=1, tiled=True),
        "sc",
        split_axis=1,
        concat_axis=4,
        tiled=True,
    )


def solution(mesh):
    return jax.shard_map(
        body,
        mesh=mesh,
        in_specs=(
            P("cell", "sc", None, "panel", None),
            P("cell", "sc", None, None, "panel"),
            P("cell"),
            P("cell", "sc"),
            P("cell", None, None),
        ),
        out_specs=P("cell", "sc", None, None, None),
        check_vma=False,
    )
```

profile of v0, /device:TPU:0, one launch (start us, length us, event | category | flops | bytes accessed | tf_op | source)
XLA Modules:
  0.0 358.8 jit_solution(6481282010595207241)
XLA Ops:
  8.7 5.1 %collective-permute-start = (bf16[2,1,2,512,128]{4,3,2,1,0:T(8,128)(2,1)}, bf16[2,1,2,512,128]{4,3,2,1,0:T(8,128)(2,1)S(1)}, u32[]{:S(2)}, u32[]{:S(2)}) collective-permute-start(bf16[2,1,2,512,128]{4,3,2,1,0:T(8,128)(2,1)} %get-tuple-element.7), channel_id=1, source_target_pairs={{0,1},{1,2},{2,3},{3,4},{4,5},{5,6},{6,7},{7,8},{8,9},{9,10},{10,1... | collective-permute-start | bytes 1572872 | tf_op jit(solution)/shard_map/ppermute | solution.py:15
  16.0 9.2 %collective-permute-done = bf16[2,1,2,512,128]{4,3,2,1,0:T(8,128)(2,1)S(1)} collective-permute-done((bf16[2,1,2,512,128]{4,3,2,1,0:T(8,128)(2,1)}, bf16[2,1,2,512,128]{4,3,2,1,0:T(8,128)(2,1)S(1)}, u32[]{:S(2)}, u32[]{:S(2)}) %collective-permute-start) | collective-permute-done | bytes 524320 | tf_op jit(solution)/shard_map/ppermute | solution.py:15
  25.3 13.1 %collective-permute-done.1 = bf16[2,1,2,512,128]{4,3,2,1,0:T(8,128)(2,1)S(1)} collective-permute-done((bf16[2,1,2,512,128]{4,3,2,1,0:T(8,128)(2,1)S(1)}, bf16[2,1,2,512,128]{4,3,2,1,0:T(8,128)(2,1)S(1)}, u32[]{:S(2)}, u32[]{:S(2)}) %collective-permute-start.1) | collective-permute-done | bytes 524320 | tf_op jit(solution)/shard_map/ppermute | solution.py:18
  38.4 26.0 %multiply_convert_fusion = bf16[2,32,2,512,128]{4,3,2,1,0:T(8,128)(2,1)} fusion(bf16[2,32,2,512,128]{4,3,2,1,0:T(8,128)(2,1)} %param.5, bf16[2,1,2,512,128]{4,3,2,1,0:T(8,128)(2,1)S(1)} %collective-permute-done.1, bf16[2,1,2,512,128]{4,3,2,1,0:T(8,128)(2,1)S(1)} %collective-permute-done, f32[2,32,128]{2,1,0:T(8,128)S(1)} %fusion.44, f32[32]{0:T(128)S(1)} %or_select_fusion), kind=kLoop, calls=%fused_computation | loop fusion | flops 109051904 | bytes 34635904 | tf_op jit(solution)/shard_map/convert_element_type | solution.py:59
  64.4 7.0 %fusion = f32[2,32,2,128,2,14]{3,5,4,2,1,0:T(8,128)S(1)} fusion(bf16[2,32,2,512,128]{4,3,2,1,0:T(8,128)(2,1)} %multiply_convert_fusion, bf16[2,32,2,14,512,1]{4,2,3,1,0,5:T(2,128)(2,1)S(1)} %bitcast.138), kind=kOutput, calls=%fused_computation.3 | convolution fusion | flops 469762048 | bytes 20447232 | tf_op jit(solution)/shard_map/cfaku,cfbsk->cfabsu/dot_general | solution.py:24
  73.9 45.8 %all-reduce.4.cloned.1.call-done = f32[2,32,2,14,128]{4,1,3,2,0:T(8,128)} async-done(((f32[2,32,2,14,128]{4,1,3,2,0:T(8,128)}), f32[2,32,2,14,128]{4,1,3,2,0:T(8,128)}) %all-reduce.4.cloned.1.call-update) | async-done | bytes 917520 | tf_op jit(solution)/shard_map/psum | solution.py:62
  120.9 14.8 %fusion.10 = f32[2,32,2,2,14,512]{5,4,2,3,1,0:T(8,128)} fusion(bf16[2,32,2,512,128]{4,3,2,1,0:T(8,128)(2,1)} %multiply_convert_fusion, bf16[2,32,2,14,128,1]{4,1,3,2,0,5:T(8,128)(2,1)S(1)} %convert_bitcast_fusion.1), kind=kOutput, calls=%fused_computation.14 | convolution fusion | flops 469762048 | bytes 24576000 | tf_op jit(solution)/shard_map/cfaku,cfbsu->cfabsk/dot_general | solution.py:32
  135.8 2.6 fusion.26
  141.0 8.2 %fusion.6 = f32[2,32,2,14,2,128]{5,3,4,2,1,0:T(8,128)S(1)} fusion(bf16[2,32,2,512,128]{4,3,2,1,0:T(8,128)(2,1)} %multiply_convert_fusion, bf16[2,32,1,14,512]{4,3,1,0,2:T(8,128)(2,1)S(1)} %fusion.27, bf16[2,32,1,14,512]{4,3,1,0,2:T(8,128)(2,1)S(1)} %fusion.26), kind=kOutput, calls=%fused_computation.9 | convolution fusion | flops 470679552 | bytes 20447232 | tf_op jit(solution)/shard_map/cfaku,cfbsk->cfabsu/dot_general | solution.py:24
  151.8 44.6 %all-reduce.6.cloned.1.call-done = f32[2,32,2,14,128]{4,1,3,2,0:T(8,128)} async-done(((f32[2,32,2,14,128]{4,1,3,2,0:T(8,128)}), f32[2,32,2,14,128]{4,1,3,2,0:T(8,128)}) %all-reduce.6.cloned.1.call-update) | async-done | bytes 917520 | tf_op jit(solution)/shard_map/psum | solution.py:69
  200.2 14.8 %fusion.13 = f32[2,32,2,2,14,512]{5,4,2,3,1,0:T(8,128)} fusion(bf16[2,32,2,512,128]{4,3,2,1,0:T(8,128)(2,1)} %multiply_convert_fusion, bf16[2,32,2,14,128,1]{4,1,3,2,0,5:T(8,128)(2,1)S(1)} %convert_bitcast_fusion), kind=kOutput, calls=%fused_computation.15 | convolution fusion | flops 469762048 | bytes 24576000 | tf_op jit(solution)/shard_map/cfaku,cfbsu->cfabsk/dot_general | solution.py:32
  220.3 8.2 %fusion.2 = f32[2,32,2,14,2,128]{5,3,4,2,1,0:T(8,128)S(1)} fusion(bf16[2,32,2,512,128]{4,3,2,1,0:T(8,128)(2,1)} %multiply_convert_fusion, bf16[2,32,1,14,512]{4,3,1,0,2:T(8,128)(2,1)S(1)} %fusion.29, bf16[2,32,1,14,512]{4,3,1,0,2:T(8,128)(2,1)S(1)} %fusion.28), kind=kOutput, calls=%fused_computation.5 | convolution fusion | flops 470679552 | bytes 20447232 | tf_op jit(solution)/shard_map/cfaku,cfbsk->cfabsu/dot_general | solution.py:24
  231.0 44.7 %all-reduce.8.cloned.1.call-done = f32[2,32,2,14,128]{4,1,3,2,0:T(8,128)} async-done(((f32[2,32,2,14,128]{4,1,3,2,0:T(8,128)}), f32[2,32,2,14,128]{4,1,3,2,0:T(8,128)}) %all-reduce.8.cloned.1.call-update) | async-done | bytes 917520 | tf_op jit(solution)/shard_map/psum | solution.py:69
  278.4 7.0 %copy.123 = bf16[2,256,2,14,32]{4,2,3,0,1:T(2,128)(2,1)} copy(bf16[2,256,2,14,32]{1,0,4,3,2:T(2,128)(2,1)S(1)} %reshape.282) | data formatting | bytes 1835008 | tf_op jit(solution)/shard_map/reshape | solution.py:90
  285.4 5.1 %reshape.292 = bf16[2,2,114688]{2,1,0:T(2,128)(2,1)S(1)} reshape(bf16[256,2,14,2,32]{4,3,2,1,0:T(2,128)(2,1)} %bitcast.141) | data formatting | bytes 1835008
  290.5 4.5 %all_to_all.23 = bf16[2,2,114688]{2,1,0:T(2,128)(2,1)S(1)} all-to-all(bf16[2,2,114688]{2,1,0:T(2,128)(2,1)S(1)} %reshape.292), channel_id=1, replica_groups=mesh['cell'=2,'panel'=2,'sc'=32] {'cell'}, dimensions={0} | all-to-all | bytes 1835008 | tf_op jit(solution)/shard_map/all_to_all | solution.py:92
  294.9 3.0 reshape.293
  297.9 6.3 %bitcast_bitcast_fusion = bf16[256,2,14,2,32]{4,3,2,1,0:T(2,128)(2,1)} fusion(bf16[256,2,14,2,32]{4,3,2,1,0:T(2,128)(2,1)} %reshape.293), kind=kLoop, calls=%fused_computation.89 | loop fusion | bytes 1835008
  304.3 5.0 %reshape.294 = bf16[32,2,7168]{2,1,0:T(2,128)(2,1)S(1)} reshape(bf16[256,2,14,2,32]{4,3,2,1,0:T(2,128)(2,1)} %bitcast_bitcast_fusion) | data formatting | bytes 1835008
  309.3 27.6 %all_to_all.24 = bf16[32,2,7168]{2,1,0:T(2,128)(2,1)S(1)} all-to-all(bf16[32,2,7168]{2,1,0:T(2,128)(2,1)S(1)} %reshape.294), channel_id=1, replica_groups=mesh['cell'=2,'panel'=2,'sc'=32] {'sc'}, dimensions={0} | all-to-all | bytes 1835008 | tf_op jit(solution)/shard_map/all_to_all | solution.py:91
  336.8 3.2 reshape.295
  340.1 2.9 copy.166
  343.0 2.8 copy.146
  345.8 6.5 %reshape.291 = bf16[2,8,2,14,1024]{4,2,3,1,0:T(2,128)(2,1)} reshape(bf16[2,8,2,14,32,32]{5,4,2,3,1,0:T(8,128)(2,1)} %copy.146) | data formatting | bytes 1835008 | tf_op jit(solution)/shard_map/all_to_all | solution.py:91
  (48 shorter events, 27.3 us)
Async XLA Ops:
  6.5 57.8 %copy-start = (bf16[2,32,2,14,512]{4,2,3,1,0:T(2,128)(2,1)S(1)}, bf16[2,32,2,14,512]{4,2,3,1,0:T(2,128)(2,1)}, u32[]{:S(2)}) copy-start(bf16[2,32,2,14,512]{4,2,3,1,0:T(2,128)(2,1)} %param.6) | copy-start | bytes 5505028
  6.5 113.2 %all-reduce.4.cloned.1.call-start = ((), (), s32[]{:S(2)}) async-start(), calls=%async_computation.2 | async-start | bytes 1835008 | tf_op jit(solution)/shard_map/psum | solution.py:62
  8.7 16.5 %collective-permute-start = (bf16[2,1,2,512,128]{4,3,2,1,0:T(8,128)(2,1)}, bf16[2,1,2,512,128]{4,3,2,1,0:T(8,128)(2,1)S(1)}, u32[]{:S(2)}, u32[]{:S(2)}) collective-permute-start(bf16[2,1,2,512,128]{4,3,2,1,0:T(8,128)(2,1)} %get-tuple-element.7), channel_id=1, source_target_pairs={{0,1},{1,2},{2,3},{3,4},{4,5},{5,6},{6,7},{7,8},{8,9},{9,10},{10,1... | collective-permute-start | bytes 1572872 | tf_op jit(solution)/shard_map/ppermute | solution.py:15
  13.8 24.6 %collective-permute-start.1 = (bf16[2,1,2,512,128]{4,3,2,1,0:T(8,128)(2,1)S(1)}, bf16[2,1,2,512,128]{4,3,2,1,0:T(8,128)(2,1)S(1)}, u32[]{:S(2)}, u32[]{:S(2)}) collective-permute-start(bf16[2,1,2,512,128]{4,3,2,1,0:T(8,128)(2,1)S(1)} %get-tuple-element.8), channel_id=1, source_target_pairs={{1,0},{2,1},{3,2},{4,3},{5,4},{6,5},{7,6},{8,7},{9,8},{10,9},{11,1... | collective-permute-start | bytes 1572872 | tf_op jit(solution)/shard_map/ppermute | solution.py:18
  73.7 122.8 %all-reduce.6.cloned.1.call-start = ((), (), s32[]{:S(2)}) async-start(), calls=%async_computation.3 | async-start | bytes 1835008 | tf_op jit(solution)/shard_map/psum | solution.py:69
  150.3 46.1 %copy-start.2 = (f32[2,32,2,14,128]{4,1,3,2,0:T(8,128)S(1)}, f32[2,32,2,14,128]{4,1,3,2,0:T(8,128)}, u32[]{:S(2)}) copy-start(f32[2,32,2,14,128]{4,1,3,2,0:T(8,128)} %all-reduce.4.cloned.1.call-done) | copy-start | bytes 2752516
  150.3 46.1 %copy-start.5 = (f32[2]{0:T(128)S(1)}, f32[2]{0:T(128)}, u32[]{:S(2)}) copy-start(f32[2]{0:T(128)} %param.7) | copy-start | bytes 28
  151.5 124.1 %all-reduce.8.cloned.1.call-start = ((), (), s32[]{:S(2)}) async-start(), calls=%async_computation.4 | async-start | bytes 1835008 | tf_op jit(solution)/shard_map/psum | solution.py:69
  196.4 3.3 copy-start.3
  229.5 1.2 copy-start.4
  343.0 9.3 %copy-start.1 = (bf16[2,32,2,14,512]{4,2,3,1,0:T(2,128)(2,1)S(1)}, bf16[2,32,2,14,512]{4,2,3,1,0:T(2,128)(2,1)}, u32[]{:S(2)}) copy-start(bf16[2,32,2,14,512]{4,2,3,1,0:T(2,128)(2,1)} %param.6) | copy-start | bytes 5505028
Sparse Core Ops, SparseCore 0:
  73.8 45.8 all-reduce.3
  151.6 44.7 all-reduce.5
  230.9 44.7 all-reduce.7
where the time goes:
time: 360 us; the launch traced here: 359 us
  waiting for transfers between devices  158 us (44%)
  matrix products  53.8 us (15%)
  local copies, waits for them, and re-layouts  48.4 us (13%)
  other arithmetic  46.9 us (13%)
  blocking collectives  32 us (9%)
  between operations  13.4 us (4%)
  starting transfers between devices  6.84 us (2%)
    psum x2, waiting for transfers between devices, body(): lax.psum(adjoint_apply(smoothed, column_image), 'panel') + noise * direction  89.4 us
    psum x1, waiting for transfers between devices, body(): matched = lax.psum(partial_sums, 'panel')  45.8 us
    dot_general x2, matrix products, apply_channel(): jnp.einsum('cfaku,cfbsu->cfabsk', matrix, vector, preferred_element_type=...  29.7 us
    all_to_all x1, blocking collectives, body(): lax.all_to_all(lax.all_to_all(outgoing, 'cell', split_axis=1, concat_axis...  27.6 us
    convert_element_type x1, other arithmetic, body(): smoothed = (smooth * active[:, :, None, None, :]).astype(jnp.bfloat16)  26 us
    dot_general x3, matrix products, adjoint_apply(): jnp.einsum('cfaku,cfbsk->cfabsu', matrix, vector, preferred_element_type=...  23.4 us
    unnamed x17, local copies, waits for them, and re-layouts  22.7 us
    ppermute x1, waiting for transfers between devices, with_halo(): lax.ppermute(lax.slice_in_dim(block, 0, width, axis=dim), axis, backward)  13.1 us
  transfers between devices with their start and end apart: 5, of which 5 were waited for; matrix products, arithmetic and copies ran while one was open for 0% of the time, Pallas kernels for 0%

commit v1 on v0

--- a/solution.py
+++ b/solution.py
@@ -66,7 +66,11 @@
     norm_now = user_sum(residual, residual)
     for iteration in range(ITERS):
         column_image = apply_channel(smoothed, direction.astype(jnp.bfloat16)).astype(jnp.bfloat16)
-        image = lax.psum(adjoint_apply(smoothed, column_image), "panel") + noise * direction
+        produce_the_strips_all = lambda inner_x, a_name: lax.all_gather(inner_x, a_name).sum(axis=0)
+        image = (
+            produce_the_strips_all(adjoint_apply(smoothed, column_image), "panel")
+            + noise * direction
+        )
         alpha = norm_now / user_sum(direction, image)
         estimate = estimate + widen(alpha) * direction
         residual = residual - widen(alpha) * image

time: 360 us -> 347 us (0.964)
  waiting for transfers between devices: 158 us -> 141 us
    psum x2 -> x0, waiting for transfers between devices: 89.4 us -> none  [body(): lax.psum(adjoint_apply(smoothed, column_image), 'panel') + noise * direction]
    all_gather x0 -> x2, waiting for transfers between devices: none -> 73 us  [body(): lax.all_gather(inner_x, a_name).sum(axis=0)]
    reduce_sum x0 -> x2, other arithmetic: none -> 4.74 us  [body(): lax.all_gather(inner_x, a_name).sum(axis=0)]
    unnamed x17 -> x15, local copies, waits for them, and re-layouts: 22.7 us -> 22.6 us
where the time goes in v1:
time: 347 us; the launch traced here: 346 us
  waiting for transfers between devices  141 us (41%)
  matrix products  54.8 us (16%)
  other arithmetic  50 us (14%)
  local copies, waits for them, and re-layouts  48.4 us (14%)
  blocking collectives  31.9 us (9%)
  between operations  13.4 us (4%)
  starting transfers between devices  6.62 us (2%)
    all_gather x2, waiting for transfers between devices, body(): lax.all_gather(inner_x, a_name).sum(axis=0)  73 us
    psum x1, waiting for transfers between devices, body(): matched = lax.psum(partial_sums, 'panel')  46 us
    dot_general x2, matrix products, apply_channel(): jnp.einsum('cfaku,cfbsu->cfabsk', matrix, vector, preferred_element_type=...  29.7 us
    all_to_all x1, blocking collectives, body(): lax.all_to_all(lax.all_to_all(outgoing, 'cell', split_axis=1, concat_axis...  27.4 us
    convert_element_type x1, other arithmetic, body(): smoothed = (smooth * active[:, :, None, None, :]).astype(jnp.bfloat16)  26 us
    dot_general x3, matrix products, adjoint_apply(): jnp.einsum('cfaku,cfbsk->cfabsu', matrix, vector, preferred_element_type=...  23.4 us
    unnamed x15, local copies, waits for them, and re-layouts  22.6 us
    ppermute x1, waiting for transfers between devices, with_halo(): lax.ppermute(lax.slice_in_dim(block, 0, width, axis=dim), axis, backward)  13.1 us
  transfers between devices with their start and end apart: 5, of which 5 were waited for; matrix products, arithmetic and copies ran while one was open for 0% of the time, Pallas kernels for 0%

profile of v1, /device:TPU:0, one launch (start us, length us, event | category | flops | bytes accessed | tf_op | source)
XLA Modules:
  0.0 346.5 jit_solution(10945824700965465879)
XLA Ops:
  8.7 5.1 %collective-permute-start = (bf16[2,1,2,512,128]{4,3,2,1,0:T(8,128)(2,1)}, bf16[2,1,2,512,128]{4,3,2,1,0:T(8,128)(2,1)S(1)}, u32[]{:S(2)}, u32[]{:S(2)}) collective-permute-start(bf16[2,1,2,512,128]{4,3,2,1,0:T(8,128)(2,1)} %get-tuple-element.7), channel_id=1, source_target_pairs={{0,1},{1,2},{2,3},{3,4},{4,5},{5,6},{6,7},{7,8},{8,9},{9,10},{10,1... | collective-permute-start | bytes 1572872 | tf_op jit(solution)/shard_map/ppermute | solution.py:15
  16.0 9.2 %collective-permute-done = bf16[2,1,2,512,128]{4,3,2,1,0:T(8,128)(2,1)S(1)} collective-permute-done((bf16[2,1,2,512,128]{4,3,2,1,0:T(8,128)(2,1)}, bf16[2,1,2,512,128]{4,3,2,1,0:T(8,128)(2,1)S(1)}, u32[]{:S(2)}, u32[]{:S(2)}) %collective-permute-start) | collective-permute-done | bytes 524320 | tf_op jit(solution)/shard_map/ppermute | solution.py:15
  25.3 13.1 %collective-permute-done.1 = bf16[2,1,2,512,128]{4,3,2,1,0:T(8,128)(2,1)S(1)} collective-permute-done((bf16[2,1,2,512,128]{4,3,2,1,0:T(8,128)(2,1)S(1)}, bf16[2,1,2,512,128]{4,3,2,1,0:T(8,128)(2,1)S(1)}, u32[]{:S(2)}, u32[]{:S(2)}) %collective-permute-start.1) | collective-permute-done | bytes 524320 | tf_op jit(solution)/shard_map/ppermute | solution.py:18
  38.4 26.0 %multiply_convert_fusion = bf16[2,32,2,512,128]{4,3,2,1,0:T(8,128)(2,1)} fusion(bf16[2,32,2,512,128]{4,3,2,1,0:T(8,128)(2,1)} %param.5, bf16[2,1,2,512,128]{4,3,2,1,0:T(8,128)(2,1)S(1)} %collective-permute-done.1, bf16[2,1,2,512,128]{4,3,2,1,0:T(8,128)(2,1)S(1)} %collective-permute-done, f32[2,32,128]{2,1,0:T(8,128)S(1)} %fusion.58, f32[32]{0:T(128)S(1)} %or_select_fusion), kind=kLoop, calls=%fused_computation | loop fusion | flops 109051904 | bytes 34635904 | tf_op jit(solution)/shard_map/convert_element_type | solution.py:59
  64.4 7.0 %fusion = f32[2,32,2,128,2,14]{3,5,4,2,1,0:T(8,128)S(1)} fusion(bf16[2,32,2,512,128]{4,3,2,1,0:T(8,128)(2,1)} %multiply_convert_fusion, bf16[2,32,2,14,512,1]{4,2,3,1,0,5:T(2,128)(2,1)S(1)} %bitcast.158), kind=kOutput, calls=%fused_computation.3 | convolution fusion | flops 469762048 | bytes 20447232 | tf_op jit(solution)/shard_map/cfaku,cfbsk->cfabsu/dot_general | solution.py:24
  73.7 46.0 %all-reduce.2.cloned.1.call-done = f32[2,32,2,14,128]{4,1,3,2,0:T(8,128)} async-done(((f32[2,32,2,14,128]{4,1,3,2,0:T(8,128)}), f32[2,32,2,14,128]{4,1,3,2,0:T(8,128)}) %all-reduce.2.cloned.1.call-update) | async-done | bytes 917520 | tf_op jit(solution)/shard_map/psum | solution.py:62
  120.9 14.8 %fusion.10 = f32[2,32,2,2,14,512]{5,4,2,3,1,0:T(8,128)} fusion(bf16[2,32,2,512,128]{4,3,2,1,0:T(8,128)(2,1)} %multiply_convert_fusion, bf16[2,32,2,14,128,1]{4,1,3,2,0,5:T(8,128)(2,1)S(1)} %convert_bitcast_fusion.1), kind=kOutput, calls=%fused_computation.14 | convolution fusion | flops 469762048 | bytes 24576000 | tf_op jit(solution)/shard_map/cfaku,cfbsu->cfabsk/dot_general | solution.py:32
  141.0 8.2 %fusion.25 = f32[2,32,2,2,14,128]{5,4,2,3,1,0:T(8,128)S(1)} fusion(bf16[2,32,2,512,128]{4,3,2,1,0:T(8,128)(2,1)} %multiply_convert_fusion, bf16[2,32,1,14,512]{4,3,1,0,2:T(8,128)(2,1)S(1)} %fusion.37, bf16[2,32,1,14,512]{4,3,1,0,2:T(8,128)(2,1)S(1)} %fusion.36), kind=kOutput, calls=%fused_computation.35 | convolution fusion | flops 470679552 | bytes 20447232 | tf_op jit(solution)/shard_map/cfaku,cfbsk->cfabsu/dot_general | solution.py:24
  150.7 36.5 %all-gather.5.cloned.1.call-done = f32[4,32,2,14,128]{4,3,1,0,2:T(8,128)} async-done(((f32[2,32,2,14,128]{4,3,1,0,2:T(8,128)}), f32[4,32,2,14,128]{4,3,1,0,2:T(8,128)}) %all-gather.5.cloned.1.call-update) | async-done | bytes 1835024 | tf_op jit(solution)/shard_map/all_gather | solution.py:69
  190.7 14.8 %fusion.13 = f32[2,32,2,2,14,512]{5,4,2,3,1,0:T(8,128)} fusion(bf16[2,32,2,512,128]{4,3,2,1,0:T(8,128)(2,1)} %multiply_convert_fusion, bf16[2,32,2,14,128,1]{4,1,3,2,0,5:T(8,128)(2,1)S(1)} %convert_bitcast_fusion), kind=kOutput, calls=%fused_computation.15 | convolution fusion | flops 469762048 | bytes 24576000 | tf_op jit(solution)/shard_map/cfaku,cfbsu->cfabsk/dot_general | solution.py:32
  210.8 8.2 %fusion.30 = f32[2,32,2,2,14,128]{5,4,2,3,1,0:T(8,128)S(1)} fusion(bf16[2,32,2,512,128]{4,3,2,1,0:T(8,128)(2,1)} %multiply_convert_fusion, bf16[2,32,1,14,512]{4,3,1,0,2:T(8,128)(2,1)S(1)} %fusion.39, bf16[2,32,1,14,512]{4,3,1,0,2:T(8,128)(2,1)S(1)} %fusion.38), kind=kOutput, calls=%fused_computation.36 | convolution fusion | flops 470679552 | bytes 20447232 | tf_op jit(solution)/shard_map/cfaku,cfbsk->cfabsu/dot_general | solution.py:24
  220.4 36.5 %all-gather.7.cloned.1.call-done = f32[4,32,2,14,128]{4,3,1,0,2:T(8,128)} async-done(((f32[2,32,2,14,128]{4,3,1,0,2:T(8,128)}), f32[4,32,2,14,128]{4,3,1,0,2:T(8,128)}) %all-gather.7.cloned.1.call-update) | async-done | bytes 1835024 | tf_op jit(solution)/shard_map/all_gather | solution.py:69
  257.0 2.9 reduce_sum.71
  266.1 7.0 %copy.157 = bf16[2,256,2,14,32]{4,2,3,0,1:T(2,128)(2,1)} copy(bf16[2,256,2,14,32]{1,0,4,3,2:T(2,128)(2,1)S(1)} %reshape.282) | data formatting | bytes 1835008 | tf_op jit(solution)/shard_map/reshape | solution.py:94
  273.2 5.1 %reshape.294 = bf16[2,2,114688]{2,1,0:T(2,128)(2,1)S(1)} reshape(bf16[256,2,14,2,32]{4,3,2,1,0:T(2,128)(2,1)} %bitcast.161) | data formatting | bytes 1835008
  278.2 4.5 %all_to_all.23 = bf16[2,2,114688]{2,1,0:T(2,128)(2,1)S(1)} all-to-all(bf16[2,2,114688]{2,1,0:T(2,128)(2,1)S(1)} %reshape.294), channel_id=1, replica_groups=mesh['cell'=2,'panel'=2,'sc'=32] {'cell'}, dimensions={0} | all-to-all | bytes 1835008 | tf_op jit(solution)/shard_map/all_to_all | solution.py:96
  282.7 3.0 reshape.295
  285.7 6.3 %bitcast_bitcast_fusion = bf16[256,2,14,2,32]{4,3,2,1,0:T(2,128)(2,1)} fusion(bf16[256,2,14,2,32]{4,3,2,1,0:T(2,128)(2,1)} %reshape.295), kind=kLoop, calls=%fused_computation.95 | loop fusion | bytes 1835008
  292.0 5.0 %reshape.296 = bf16[32,2,7168]{2,1,0:T(2,128)(2,1)S(1)} reshape(bf16[256,2,14,2,32]{4,3,2,1,0:T(2,128)(2,1)} %bitcast_bitcast_fusion) | data formatting | bytes 1835008
  297.0 27.4 %all_to_all.24 = bf16[32,2,7168]{2,1,0:T(2,128)(2,1)S(1)} all-to-all(bf16[32,2,7168]{2,1,0:T(2,128)(2,1)S(1)} %reshape.296), channel_id=1, replica_groups=mesh['cell'=2,'panel'=2,'sc'=32] {'sc'}, dimensions={0} | all-to-all | bytes 1835008 | tf_op jit(solution)/shard_map/all_to_all | solution.py:95
  324.4 3.2 reshape.297
  327.7 2.9 copy.227
  330.6 2.8 copy.180
  333.4 6.5 %reshape.293 = bf16[2,8,2,14,1024]{4,2,3,1,0:T(2,128)(2,1)} reshape(bf16[2,8,2,14,32,32]{5,4,2,3,1,0:T(8,128)(2,1)} %copy.180) | data formatting | bytes 1835008 | tf_op jit(solution)/shard_map/all_to_all | solution.py:95
  (48 shorter events, 31.0 us)
Async XLA Ops:
  6.5 57.8 %copy-start = (bf16[2,32,2,14,512]{4,2,3,1,0:T(2,128)(2,1)S(1)}, bf16[2,32,2,14,512]{4,2,3,1,0:T(2,128)(2,1)}, u32[]{:S(2)}) copy-start(bf16[2,32,2,14,512]{4,2,3,1,0:T(2,128)(2,1)} %param.6) | copy-start | bytes 5505028
  6.5 113.2 %all-reduce.2.cloned.1.call-start = ((), (), s32[]{:S(2)}) async-start(), calls=%async_computation.2 | async-start | bytes 1835008 | tf_op jit(solution)/shard_map/psum | solution.py:62
  8.7 16.5 %collective-permute-start = (bf16[2,1,2,512,128]{4,3,2,1,0:T(8,128)(2,1)}, bf16[2,1,2,512,128]{4,3,2,1,0:T(8,128)(2,1)S(1)}, u32[]{:S(2)}, u32[]{:S(2)}) collective-permute-start(bf16[2,1,2,512,128]{4,3,2,1,0:T(8,128)(2,1)} %get-tuple-element.7), channel_id=1, source_target_pairs={{0,1},{1,2},{2,3},{3,4},{4,5},{5,6},{6,7},{7,8},{8,9},{9,10},{10,1... | collective-permute-start | bytes 1572872 | tf_op jit(solution)/shard_map/ppermute | solution.py:15
  13.8 24.6 %collective-permute-start.1 = (bf16[2,1,2,512,128]{4,3,2,1,0:T(8,128)(2,1)S(1)}, bf16[2,1,2,512,128]{4,3,2,1,0:T(8,128)(2,1)S(1)}, u32[]{:S(2)}, u32[]{:S(2)}) collective-permute-start(bf16[2,1,2,512,128]{4,3,2,1,0:T(8,128)(2,1)S(1)} %get-tuple-element.8), channel_id=1, source_target_pairs={{1,0},{2,1},{3,2},{4,3},{5,4},{6,5},{7,6},{8,7},{9,8},{10,9},{11,1... | collective-permute-start | bytes 1572872 | tf_op jit(solution)/shard_map/ppermute | solution.py:18
  73.7 113.6 %all-gather.5.cloned.1.call-start = ((), (), s32[]{:S(2)}) async-start(), calls=%async_computation.3 | async-start | bytes 3145728 | tf_op jit(solution)/shard_map/all_gather | solution.py:69
  149.3 39.8 %copy-start.2 = (f32[2,32,2,14,128]{4,1,3,2,0:T(8,128)S(1)}, f32[2,32,2,14,128]{4,1,3,2,0:T(8,128)}, u32[]{:S(2)}) copy-start(f32[2,32,2,14,128]{4,1,3,2,0:T(8,128)} %all-reduce.2.cloned.1.call-done) | copy-start | bytes 2752516
  149.3 39.8 %copy-start.4 = (f32[2]{0:T(128)S(1)}, f32[2]{0:T(128)}, u32[]{:S(2)}) copy-start(f32[2]{0:T(128)} %param.7) | copy-start | bytes 28
  150.5 106.5 %all-gather.7.cloned.1.call-start = ((), (), s32[]{:S(2)}) async-start(), calls=%async_computation.4 | async-start | bytes 3145728 | tf_op jit(solution)/shard_map/all_gather | solution.py:69
  219.0 1.2 copy-start.3
  330.6 9.3 %copy-start.1 = (bf16[2,32,2,14,512]{4,2,3,1,0:T(2,128)(2,1)S(1)}, bf16[2,32,2,14,512]{4,2,3,1,0:T(2,128)(2,1)}, u32[]{:S(2)}) copy-start(bf16[2,32,2,14,512]{4,2,3,1,0:T(2,128)(2,1)} %param.6) | copy-start | bytes 5505028
Sparse Core Ops, SparseCore 0:
  73.8 45.8 all-reduce.1
  150.6 36.5 all-gather.4
  220.4 36.5 all-gather.6
